TPU v7x, 256 devices: a whole 4x4x8 slice. The times are simulated.
256 devices in a mesh: tm: 8 (over y, core), head: 32 (over z, x).
Axes of the slice: x: 4, y: 4, z: 8, core: 2. Of those that a mesh axis runs over, the one named last changes fastest.
Arguments:
- tokens: bfloat16 [4096, 5120], P('tm'), may hold values from -24 to 24
- w_query: bfloat16 [5120, 4096], P(None, 'head'), may hold values from -0.078125 to 0.078125
- w_key: bfloat16 [5120, 4096], P(None, 'head'), may hold values from -0.078125 to 0.078125
- w_value: bfloat16 [5120, 4096], P(None, 'head'), may hold values from -0.078125 to 0.078125
- w_out: bfloat16 [4096, 5120], P('head'), may hold values from -0.09375 to 0.09375
- out_grad: bfloat16 [4096, 5120], P('tm'), may hold values from -6 to 6
- frame_lists: int32 [8, 8], replicated, may hold values from 0 to 1, as said below
Outputs:
- token_grad: bfloat16 [4096, 5120], P(('tm', 'head'))
- query_grad: bfloat16 [5120, 4096], P('tm', 'head')
- key_grad: bfloat16 [5120, 4096], P('tm', 'head')
- value_grad: bfloat16 [5120, 4096], P('tm', 'head')
- out_weight_grad: bfloat16 [4096, 5120], P('head', 'tm')
Inputs may be any that keep to these rules, and one draw needn't show every extreme that they name: `frame_lists`: entries with j >= i are 0; entry (i, i - 1) is 1 for every group i > 0.
All inputs are finite; a program needn't handle non-finite values.
Results may differ from a plain program's by a relative error of at most 0.02.
The roundings to bfloat16 on the way count: a program that leaves them out, or rounds other values in their place, can miss the bound.
Values may be sent and summed in bfloat16 or wider, within the bound.
A program may use at most 128 MiB of HBM per device.

v0:
```python
import jax
import jax.numpy as jnp
from jax import lax
from jax.sharding import PartitionSpec as P


def contract_rows(left, right):
    return lax.dot_general(
        left, right, (((0,), (0,)), ((), ())), preferred_element_type=jnp.float32
    )


def contract_cols(left, right):
    return lax.dot_general(
        left, right, (((1,), (1,)), ((), ())), preferred_element_type=jnp.float32
    )


def local(tokens, w_query, w_key, w_value, w_out, out_grad, frame_lists):
    width = w_query.shape[1]
    scale = 1.0 / width**0.5
    rows = tokens.shape[0]
    groups = lax.axis_size("tm")
    mine = lax.axis_index("tm")
    query = jnp.dot(tokens, w_query, preferred_element_type=jnp.float32).astype(jnp.bfloat16)
    keys = jnp.dot(tokens, w_key, preferred_element_type=jnp.float32).astype(jnp.bfloat16)
    values = jnp.dot(tokens, w_value, preferred_element_type=jnp.float32).astype(jnp.bfloat16)
    d_attn = contract_cols(out_grad, w_out).astype(jnp.bfloat16)
    my_list = lax.dynamic_slice_in_dim(frame_lists, mine, 1, 0)[0]
    key_all, value_all = (
        lax.all_gather(keys, "tm", axis=0, tiled=True),
        lax.all_gather(values, "tm", axis=0, tiled=True),
    )
    order = jnp.arange(groups, dtype=jnp.int32)
    allowed = (order == mine) | (my_list == 1) & (order < mine)
    key_mask = jnp.repeat(allowed, rows)[None, :]
    scores = contract_cols(query, key_all) * scale
    scores = jnp.where(key_mask, scores, jnp.float32(-1e30))
    top = jnp.max(scores, axis=1, keepdims=True)
    expd = jnp.exp(scores - top)
    probs = expd / jnp.sum(expd, axis=1, keepdims=True)
    probs_b = probs.astype(jnp.bfloat16)
    attn = jnp.dot(probs_b, value_all, preferred_element_type=jnp.float32).astype(jnp.bfloat16)
    dprobs = contract_cols(d_attn, value_all)
    delta = jnp.sum(probs * dprobs, axis=1, keepdims=True)
    dscore = (probs * (dprobs - delta) * scale).astype(jnp.bfloat16)
    dquery = jnp.dot(dscore, key_all, preferred_element_type=jnp.float32).astype(jnp.bfloat16)
    cache_terms = jnp.concatenate(
        [contract_rows(dscore, query), contract_rows(probs_b, d_attn)], axis=1
    )
    summed = lax.psum_scatter(
        cache_terms.astype(jnp.bfloat16), "tm", scatter_dimension=0, tiled=True
    ).astype(jnp.float32)
    dkey = summed[:, :width].astype(jnp.bfloat16)
    dvalue = summed[:, width:].astype(jnp.bfloat16)
    weights_sum = lax.psum_scatter(
        jnp.concatenate(
            [
                contract_rows(tokens, dquery),
                contract_rows(tokens, dkey),
                contract_rows(tokens, dvalue),
                contract_rows(out_grad, attn),
            ],
            axis=1,
        ).astype(jnp.bfloat16),
        "tm",
        scatter_dimension=0,
        tiled=True,
    ).astype(jnp.float32)
    query_grad = weights_sum[:, :width].astype(jnp.bfloat16)
    key_grad = weights_sum[:, width : 2 * width].astype(jnp.bfloat16)
    value_grad = weights_sum[:, 2 * width : 3 * width].astype(jnp.bfloat16)
    out_weight_grad = weights_sum[:, 3 * width :].T.astype(jnp.bfloat16)
    token_grad = lax.psum_scatter(
        (
            contract_cols(dquery, w_query)
            + contract_cols(dkey, w_key)
            + contract_cols(dvalue, w_value)
        ).astype(jnp.bfloat16),
        "head",
        scatter_dimension=0,
        tiled=True,
    )
    return (token_grad, query_grad, key_grad, value_grad, out_weight_grad)


def solution(mesh):
    in_specs = (
        P("tm", None),
        P(None, "head"),
        P(None, "head"),
        P(None, "head"),
        P("head", None),
        P("tm", None),
        P(),
    )
    out_specs = (
        P(("tm", "head"), None),
        P("tm", "head"),
        P("tm", "head"),
        P("tm", "head"),
        P("head", "tm"),
    )
    return jax.shard_map(local, mesh=mesh, in_specs=in_specs, out_specs=out_specs, check_vma=False)
```

profile of v0, /device:TPU:8, one launch (start us, length us, event | category | flops | bytes accessed | tf_op | source)
XLA Modules:
  0.0 424.9 jit_solution(9849481897770291235)
XLA Ops:
  7.2 0.0 copy-start
  7.2 0.0 copy-start.7
  7.2 0.0 all-gather.3.cloned.1.call-start
  7.2 5.2 %convolution_convert_fusion.9 = bf16[512,128]{1,0:T(8,128)(2,1)} fusion(bf16[512,5120]{1,0:T(8,128)(2,1)} %param.7, bf16[5120,128]{1,0:T(8,128)(2,1)} %param.9), kind=kOutput, calls=%fused_computation.26 | convolution fusion | flops 671154176 | bytes 6684672 | tf_op jit(solution)/shard_map/dot_general | solution.py:26
  12.4 0.0 all-gather.3.cloned.1.call-update
  12.5 0.0 all-gather.5.cloned.1.call-start
  12.5 0.0 copy-done.7
  12.5 4.7 %convolution_convert_fusion.7 = bf16[512,128]{1,0:T(8,128)(2,1)} fusion(bf16[512,5120]{1,0:T(8,128)(2,1)} %param.7, bf16[5120,128]{1,0:T(8,128)(2,1)S(1)} %copy-done.7), kind=kOutput, calls=%fused_computation.24 | convolution fusion | flops 671154176 | bytes 6684672 | tf_op jit(solution)/shard_map/dot_general | solution.py:27
  17.2 0.0 all-gather.5.cloned.1.call-update
  17.2 0.0 reduce-scatter.6.cloned.1.call-start
  17.3 0.8 fusion.20
  18.0 0.1 broadcast_bitcast_fusion
  18.1 4.0 convolution_convert_fusion.10
  22.2 4.0 convolution_convert_fusion.8
  26.2 13.5 %all-gather.3.cloned.1.call-done = bf16[4096,128]{1,0:T(8,128)(2,1)} async-done(((bf16[512,128]{1,0:T(8,128)(2,1)}), bf16[4096,128]{1,0:T(8,128)(2,1)}) %all-gather.3.cloned.1.call-update) | async-done | bytes 1048592 | tf_op jit(solution)/shard_map/all_gather | solution.py:31
  39.7 2.7 fusion
  42.5 3.2 copy-done.2
  45.7 2.2 fusion.2
  47.9 20.2 %all-gather.5.cloned.1.call-done = bf16[4096,128]{1,0:T(8,128)(2,1)} async-done(((bf16[512,128]{1,0:T(8,128)(2,1)}), bf16[4096,128]{1,0:T(8,128)(2,1)}) %all-gather.5.cloned.1.call-update) | async-done | bytes 1048592 | tf_op jit(solution)/shard_map/all_gather | solution.py:32
  68.0 7.4 %multiply_reduce_fusion = (f32[512]{0:T(512)S(1)}, f32[512,4096]{1,0:T(8,128)S(1)}, f32[512,4096]{1,0:T(8,128)}) fusion(f32[512]{0:T(512)S(1)} %fusion.2, f32[512]{0:T(512)S(1)} %get-tuple-element.21, f32[512,4096]{1,0:T(8,128)} %copy-done.2, pred[4096]{0:T(1024)(128)(4,1)S(1)} %bitcast.47, bf16[512,128]{1,0:T(8,128)(2,1)S(1)} %convolution_convert_fusion.8, ...), kind=kOutput, calls=%fused_computation.2 | convolution fusion | flops 549453312 | bytes 26355712 | tf_op jit(solution)/shard_map/dot_general | solution.py:14
  75.5 0.8 convolution_convert_fusion.4
  76.2 2.5 copy-done.1
  78.7 8.0 %multiply_convert_fusion = bf16[512,4096]{1,0:T(8,128)(2,1)S(1)} fusion(f32[512,4096]{1,0:T(8,128)} %copy-done.1, f32[512,4096]{1,0:T(8,128)} %get-tuple-element.23, f32[512]{0:T(512)S(1)} %get-tuple-element.15), kind=kLoop, calls=%fused_computation.1 | loop fusion | flops 8388608 | bytes 20973568 | tf_op jit(solution)/shard_map/convert_element_type | solution.py:46
  86.7 2.0 copy-done.3
  88.7 0.8 convolution_convert_fusion.5
  89.5 1.5 pad_maximum_fusion.1
  90.9 0.0 reduce-scatter.6.cloned.1.call-update
  91.0 0.2 reduce-scatter.10.cloned.1.call-start
  91.2 3.7 convolution_convert_fusion.6
  94.9 3.4 fusion.3
  98.3 9.7 %fusion.6 = bf16[5120,128]{0,1:T(8,128)(2,1)} fusion(bf16[512,5120]{1,0:T(8,128)(2,1)} %param.12, bf16[4096,128]{1,0:T(8,128)(2,1)} %all-gather.5.cloned.1.call-done, f32[512,4096]{1,0:T(8,128)} %copy-done.1), kind=kOutput, calls=%fused_computation.15 | convolution fusion | flops 1210777600 | bytes 15990784 | tf_op jit(solution)/shard_map/dot_general | solution.py:8
  108.0 17.6 %reduce-scatter.6.cloned.1.call-done = bf16[512,256]{0,1:T(8,128)(2,1)} async-done(((bf16[4096,256]{0,1:T(8,128)(2,1)}), bf16[512,256]{0,1:T(8,128)(2,1)}) %reduce-scatter.6.cloned.1.call-update) | async-done | bytes 262160 | tf_op jit(solution)/shard_map/reduce_scatter | solution.py:51
  125.6 3.5 fusion.4
  129.1 3.4 fusion.5
  132.6 3.5 pad_maximum_fusion
  136.1 7.9 %copy.18 = bf16[5120,512]{1,0:T(8,128)(2,1)} copy(bf16[5120,512]{0,1:T(8,128)(2,1)} %pad_maximum_fusion) | data formatting | bytes 10485760
  144.0 0.0 reduce-scatter.10.cloned.1.call-update
  144.0 0.0 copy-start.6
  144.0 0.0 reduce-scatter.8.cloned.1.call-start
  144.1 1.5 fusion.23
  145.6 0.0 copy-start.8
  145.6 5.5 %fusion.18 = f32[512,5120]{1,0:T(8,128)} fusion(bf16[5120,128]{1,0:T(8,128)(2,1)S(1)} %copy-done.6, bf16[512,256]{0,1:T(8,128)(2,1)S(1)} %copy-done.5), kind=kOutput, calls=%fused_computation.32 | convolution fusion | flops 671088640 | bytes 11927552 | tf_op jit(solution)/shard_map/dot_general | solution.py:14
  151.2 8.2 %add_convert_fusion = bf16[512,5120]{1,0:T(8,128)(2,1)} fusion(f32[512,5120]{1,0:T(8,128)S(1)} %fusion.23, f32[512,5120]{1,0:T(8,128)} %fusion.18, bf16[5120,128]{1,0:T(8,128)(2,1)S(1)} %copy-done.8, bf16[512,256]{0,1:T(8,128)(2,1)S(1)} %copy-done.5), kind=kOutput, calls=%fused_computation | convolution fusion | flops 678952960 | bytes 27656192 | tf_op jit(solution)/shard_map/dot_general | solution.py:14
  159.3 0.0 reduce-scatter.8.cloned.1.call-update
  159.4 25.7 %reduce-scatter.10.cloned.1.call-done = bf16[640,512]{1,0:T(8,128)(2,1)} async-done(((bf16[5120,512]{1,0:T(8,128)(2,1)}), bf16[640,512]{1,0:T(8,128)(2,1)}) %reduce-scatter.10.cloned.1.call-update) | async-done | bytes 655376
  185.1 2.0 fusion.22
  187.0 0.8 copy.23
  187.8 230.5 %reduce-scatter.8.cloned.1.call-done = bf16[16,5120]{1,0:T(8,128)(2,1)} async-done(((bf16[512,5120]{1,0:T(8,128)(2,1)}), bf16[16,5120]{1,0:T(8,128)(2,1)}) %reduce-scatter.8.cloned.1.call-update) | async-done | bytes 163856 | tf_op jit(solution)/shard_map/reduce_scatter | solution.py:74
  (13 shorter events, 0.0 us)
Async XLA Ops:
  7.2 11.0 %copy-start = (bf16[5120,128]{1,0:T(8,128)(2,1)S(1)}, bf16[5120,128]{1,0:T(8,128)(2,1)}, u32[]{:S(2)}) copy-start(bf16[5120,128]{1,0:T(8,128)(2,1)} %param.8) | copy-start | bytes 3932164
  7.2 5.3 %copy-start.7 = (bf16[5120,128]{1,0:T(8,128)(2,1)S(1)}, bf16[5120,128]{1,0:T(8,128)(2,1)}, u32[]{:S(2)}) copy-start(bf16[5120,128]{1,0:T(8,128)(2,1)} %param.10) | copy-start | bytes 3932164
  7.2 32.6 %all-gather.3.cloned.1.call-start = ((), (), s32[]{:S(2)}) async-start(), calls=%async_computation.3 | async-start | bytes 1179648 | tf_op jit(solution)/shard_map/all_gather | solution.py:31
  12.5 55.6 %all-gather.5.cloned.1.call-start = ((), (), s32[]{:S(2)}) async-start(), calls=%async_computation.4 | async-start | bytes 1179648 | tf_op jit(solution)/shard_map/all_gather | solution.py:32
  17.2 5.0 %copy-start.9 = (bf16[128,5120]{1,0:T(8,128)(2,1)S(1)}, bf16[128,5120]{1,0:T(8,128)(2,1)}, u32[]{:S(2)}) copy-start(bf16[128,5120]{1,0:T(8,128)(2,1)} %param.11) | copy-start | bytes 3932164
  17.2 108.4 %reduce-scatter.6.cloned.1.call-start = ((), (), s32[]{:S(2)}) async-start(), calls=%async_computation.5 | async-start | bytes 2359296 | tf_op jit(solution)/shard_map/reduce_scatter | solution.py:51
  42.5 3.2 copy-start.2
  75.4 3.2 copy-start.1
  86.7 2.0 copy-start.3
  91.0 94.1 %reduce-scatter.10.cloned.1.call-start = ((), (), s32[]{:S(2)}) async-start(), calls=%async_computation.7 | async-start | bytes 5898240
  125.6 3.5 copy-start.5
  129.1 3.5 copy-start.4
  144.0 1.6 copy-start.6
  144.0 274.3 %reduce-scatter.8.cloned.1.call-start = ((), (), s32[]{:S(2)}) async-start(), calls=%async_computation.6 | async-start | bytes 5406720 | tf_op jit(solution)/shard_map/reduce_scatter | solution.py:74
  145.6 5.5 %copy-start.8 = (bf16[5120,128]{1,0:T(8,128)(2,1)S(1)}, bf16[5120,128]{1,0:T(8,128)(2,1)}, u32[]{:S(2)}) copy-start(bf16[5120,128]{1,0:T(8,128)(2,1)} %param.10) | copy-start | bytes 3932164
Sparse Core Ops, SparseCore 0:
  12.6 27.1 all-gather.2
  42.2 25.7 all-gather.4
  91.1 34.4 reduce-scatter.5
  144.1 40.9 reduce-scatter.9
  189.5 228.8 reduce-scatter.7
where the time goes:
time: 425 us
  waiting for transfers between devices  308 us (72%)
  matrix products  68.5 us (16%)
  local copies, waits for them, and re-layouts  18.5 us (4%)
  other arithmetic  16 us (4%)
  between operations  14 us (3%)
    reduce_scatter x1, waiting for transfers between devices, local(): lax.psum_scatter((contract_cols(dquery, w_query) + contract_cols(dkey, w_...  231 us
    dot_general x6, matrix products, contract_cols(): lax.dot_general(left, right, (((1,), (1,)), ((), ())), preferred_element_...  29.4 us
    unnamed x6, waiting for transfers between devices  25.8 us
    dot_general x6, matrix products, contract_rows(): lax.dot_general(left, right, (((0,), (0,)), ((), ())), preferred_element_...  21.5 us
    all_gather x1, waiting for transfers between devices, local(): lax.all_gather(values, 'tm', axis=0, tiled=True)  20.2 us
    reduce_scatter x1, waiting for transfers between devices, local(): lax.psum_scatter(cache_terms.astype(jnp.bfloat16), 'tm', scatter_dimensio...  17.6 us
    unnamed x24, local copies, waits for them, and re-layouts  16.5 us
    all_gather x1, waiting for transfers between devices, local(): lax.all_gather(keys, 'tm', axis=0, tiled=True)  13.5 us
  transfers between devices with their start and end apart: 5, of which 5 were waited for; matrix products, arithmetic and copies ran while one was open for 13% of the time, Pallas kernels for 0%

commit v1 on v0

--- a/solution.py
+++ b/solution.py
@@ -2,6 +2,12 @@
 import jax.numpy as jnp
 from jax import lax
 from jax.sharding import PartitionSpec as P
+
+
+def change_keys(packet, dim_at):
+    t1 = list(packet.shape[1:])
+    t1[dim_at] *= packet.shape[0]
+    return jnp.moveaxis(packet, 0, dim_at).reshape(t1)
 
 
 def contract_rows(left, right):
@@ -27,9 +33,29 @@
     values = jnp.dot(tokens, w_value, preferred_element_type=jnp.float32).astype(jnp.bfloat16)
     d_attn = contract_cols(out_grad, w_out).astype(jnp.bfloat16)
     my_list = lax.dynamic_slice_in_dim(frame_lists, mine, 1, 0)[0]
+
+    def find_paths(dimension_no, load, link_axis):
+        devs = lax.axis_size(link_axis)
+        by_rank = tuple(((u, (u + 1) % devs) for u in range(devs)))
+        high, k_now = ([], [])
+        line_up = tuple(((nth, j) for j, nth in by_rank))
+        for dev_j in range(devs - 1):
+            if dev_j % 2 == 0:
+                base_arr = lax.ppermute(high[-1] if high else load, link_axis, by_rank)
+                high.append(base_arr)
+            else:
+                z = lax.ppermute(k_now[-1] if k_now else load, link_axis, line_up)
+                k_now.append(z)
+        all_rows = jnp.stack([*high[::-1], load, *k_now])
+        new = len(high)
+        s_next = lax.axis_index(link_axis)
+        last = s_next - new
+        all_rows = all_rows[(jnp.arange(devs) - last) % devs]
+        return change_keys(all_rows, dimension_no)
+
     key_all, value_all = (
         lax.all_gather(keys, "tm", axis=0, tiled=True),
-        lax.all_gather(values, "tm", axis=0, tiled=True),
+        find_paths(0, values, "tm"),
     )
     order = jnp.arange(groups, dtype=jnp.int32)
     allowed = (order == mine) | (my_list == 1) & (order < mine)

time: 425 us -> 404 us (0.951)
  waiting for transfers between devices: 308 us -> 285 us
  starting transfers between devices: 0.39 us -> 6.12 us
  matrix products: 68.5 us -> 63.9 us
    all_gather x1 -> x0, waiting for transfers between devices: 20.2 us -> none  [local(): lax.all_gather(values, 'tm', axis=0, tiled=True)]
    all_gather x1, waiting for transfers between devices: 13.5 us -> 5.61 us  [local(): lax.all_gather(keys, 'tm', axis=0, tiled=True)]
    ppermute x0 -> x7, waiting for transfers between devices: none -> 5.78 us  [the longest x4 5.77 us: find_paths(): base_arr = lax.ppermute(high[-1] if high else load, link_axis, by_rank)]
    ppermute x0 -> x7, starting transfers between devices: none -> 5.56 us  [the longest x3 3.34 us: find_paths(): z = lax.ppermute(k_now[-1] if k_now else load, link_axis, line_up)]
    unnamed x24 -> x41, local copies, waits for them, and re-layouts: 16.5 us -> 15.3 us
    unnamed x6 -> x5, waiting for transfers between devices: 25.8 us -> 25.8 us
  transfers between devices with their start and end apart: 5 -> 11, of which waited for: 5 -> 6; matrix products, arithmetic and copies ran while one was open for 13% -> 12% of each run, Pallas kernels for 0% -> 0%
where the time goes in v1:
time: 404 us; the launch traced here: 403 us
  waiting for transfers between devices  285 us (71%)
  matrix products  63.9 us (16%)
  local copies, waits for them, and re-layouts  18 us (4%)
  other arithmetic  15.9 us (4%)
  between operations  14.1 us (3%)
  starting transfers between devices  6.12 us (2%)
    reduce_scatter x1, waiting for transfers between devices, local(): lax.psum_scatter((contract_cols(dquery, w_query) + contract_cols(dkey, w_...  231 us
    dot_general x6, matrix products, contract_cols(): lax.dot_general(left, right, (((1,), (1,)), ((), ())), preferred_element_...  27.9 us
    unnamed x5, waiting for transfers between devices  25.8 us
    dot_general x6, matrix products, contract_rows(): lax.dot_general(left, right, (((0,), (0,)), ((), ())), preferred_element_...  21.5 us
    reduce_scatter x1, waiting for transfers between devices, local(): lax.psum_scatter(cache_terms.astype(jnp.bfloat16), 'tm', scatter_dimensio...  17.2 us
    unnamed x41, local copies, waits for them, and re-layouts  15.3 us
  transfers between devices with their start and end apart: 11, of which 6 were waited for; matrix products, arithmetic and copies ran while one was open for 12% of the time, Pallas kernels for 0%

profile of v1, /device:TPU:8, one launch (start us, length us, event | category | flops | bytes accessed | tf_op | source)
XLA Modules:
  0.0 403.1 jit_solution(17717103811741951310)
XLA Ops:
  7.2 0.0 all-gather.2.cloned.1.call-start
  7.2 4.5 %convolution_convert_fusion.7 = bf16[512,128]{1,0:T(8,128)(2,1)S(1)} fusion(bf16[512,5120]{1,0:T(8,128)(2,1)} %param.7, bf16[5120,128]{1,0:T(8,128)(2,1)} %param.10), kind=kOutput, calls=%fused_computation.25 | convolution fusion | flops 671154176 | bytes 6684672 | tf_op jit(solution)/shard_map/dot_general | solution.py:33
  11.8 0.0 collective-permute-start.4
  11.8 0.5 collective-permute-start
  12.3 2.2 convolution_convert_fusion.9
  14.5 0.0 all-gather.2.cloned.1.call-update
  14.5 0.2 reduce-scatter.6.cloned.1.call-start
  14.8 4.0 convolution_convert_fusion.10
  18.8 1.2 collective-permute-start.1
  20.1 5.0 %convolution_convert_fusion.8 = bf16[512,128]{1,0:T(8,128)(2,1)} fusion(bf16[512,5120]{1,0:T(8,128)(2,1)} %param.12, bf16[128,5120]{1,0:T(8,128)(2,1)} %param.11), kind=kOutput, calls=%fused_computation.26 | convolution fusion | flops 671154176 | bytes 6684672 | tf_op jit(solution)/shard_map/dot_general | solution.py:20
  25.1 0.7 fusion.20
  25.8 0.5 collective-permute-start.2
  26.3 0.1 broadcast_bitcast_fusion
  26.4 1.3 collective-permute-start.5
  27.6 2.6 collective-permute-done.2
  30.3 2.1 collective-permute-start.6
  32.3 3.2 collective-permute-done.3
  35.6 0.9 bitcast_dynamic-update-slice_fusion.4
  36.6 0.9 bitcast_dynamic-update-slice_fusion.2
  37.6 0.7 gather_fusion
  38.3 5.6 %all-gather.2.cloned.1.call-done = bf16[4096,128]{1,0:T(8,128)(2,1)} async-done(((bf16[512,128]{1,0:T(8,128)(2,1)}), bf16[4096,128]{1,0:T(8,128)(2,1)}) %all-gather.2.cloned.1.call-update) | async-done | bytes 1048592 | tf_op jit(solution)/shard_map/all_gather | solution.py:57
  43.9 2.7 fusion
  46.7 2.2 fusion.2
  48.8 4.9 %multiply_reduce_fusion = (f32[512]{0:T(512)S(1)}, f32[512,4096]{1,0:T(8,128)S(1)}, f32[512,4096]{1,0:T(8,128)}) fusion(f32[512]{0:T(512)S(1)} %fusion.2, f32[512]{0:T(512)S(1)} %get-tuple-element.21, f32[512,4096]{1,0:T(8,128)S(1)} %get-tuple-element.22, pred[4096]{0:T(1024)(128)(4,1)S(1)} %bitcast.68, bf16[512,128]{1,0:T(8,128)(2,1)S(1)} %copy-done.10, ...), kind=kOutput, calls=%fused_computation.3 | convolution fusion | flops 549453312 | bytes 26355712 | tf_op jit(solution)/shard_map/dot_general | solution.py:20
  53.7 0.8 convolution_convert_fusion.4
  54.5 2.5 copy-done.1
  57.0 8.0 %multiply_convert_fusion = bf16[512,4096]{1,0:T(8,128)(2,1)S(1)} fusion(f32[512,4096]{1,0:T(8,128)} %copy-done.1, f32[512,4096]{1,0:T(8,128)} %get-tuple-element.23, f32[512]{0:T(512)S(1)} %get-tuple-element.15), kind=kLoop, calls=%fused_computation.2 | loop fusion | flops 8388608 | bytes 20973568 | tf_op jit(solution)/shard_map/convert_element_type | solution.py:72
  65.0 2.0 copy-done.3
  67.0 0.8 convolution_convert_fusion.5
  67.8 1.5 pad_maximum_fusion.1
  69.3 0.0 reduce-scatter.6.cloned.1.call-update
  69.3 0.3 reduce-scatter.10.cloned.1.call-start
  69.6 3.7 convolution_convert_fusion.6
  73.3 3.4 fusion.3
  76.7 9.7 %fusion.6 = bf16[5120,128]{0,1:T(8,128)(2,1)} fusion(bf16[512,5120]{1,0:T(8,128)(2,1)} %param.12, bf16[4096,128]{1,0:T(8,128)(2,1)} %bitcast.64, f32[512,4096]{1,0:T(8,128)} %copy-done.1), kind=kOutput, calls=%fused_computation.16 | convolution fusion | flops 1210777600 | bytes 15990784 | tf_op jit(solution)/shard_map/dot_general | solution.py:14
  86.4 17.2 %reduce-scatter.6.cloned.1.call-done = bf16[512,256]{0,1:T(8,128)(2,1)} async-done(((bf16[4096,256]{0,1:T(8,128)(2,1)}), bf16[512,256]{0,1:T(8,128)(2,1)}) %reduce-scatter.6.cloned.1.call-update) | async-done | bytes 262160 | tf_op jit(solution)/shard_map/reduce_scatter | solution.py:77
  103.6 3.5 fusion.4
  107.1 3.4 fusion.5
  110.5 3.5 pad_maximum_fusion
  114.0 8.0 %copy.18 = bf16[5120,512]{1,0:T(8,128)(2,1)} copy(bf16[5120,512]{0,1:T(8,128)(2,1)} %pad_maximum_fusion) | data formatting | bytes 10485760
  122.0 0.0 reduce-scatter.8.cloned.1.call-start
  122.1 1.5 fusion.25
  123.6 5.6 %fusion.18 = f32[512,5120]{1,0:T(8,128)} fusion(bf16[5120,128]{1,0:T(8,128)(2,1)S(1)} %copy-done.8, bf16[512,256]{0,1:T(8,128)(2,1)S(1)} %copy-done.6), kind=kOutput, calls=%fused_computation.41 | convolution fusion | flops 671088640 | bytes 11927552 | tf_op jit(solution)/shard_map/dot_general | solution.py:20
  129.2 8.2 %add_convert_fusion = bf16[512,5120]{1,0:T(8,128)(2,1)} fusion(f32[512,5120]{1,0:T(8,128)S(1)} %fusion.25, f32[512,5120]{1,0:T(8,128)} %fusion.18, bf16[5120,128]{1,0:T(8,128)(2,1)S(1)} %copy-done.9, bf16[512,256]{0,1:T(8,128)(2,1)S(1)} %copy-done.6), kind=kOutput, calls=%fused_computation.1 | convolution fusion | flops 678952960 | bytes 27656192 | tf_op jit(solution)/shard_map/dot_general | solution.py:20
  137.4 25.7 %reduce-scatter.10.cloned.1.call-done = bf16[640,512]{1,0:T(8,128)(2,1)} async-done(((bf16[5120,512]{1,0:T(8,128)(2,1)}), bf16[640,512]{1,0:T(8,128)(2,1)}) %reduce-scatter.10.cloned.1.call-update) | async-done | bytes 655376
  163.1 2.0 fusion.24
  165.0 0.8 copy.23
  165.8 230.7 %reduce-scatter.8.cloned.1.call-done = bf16[16,5120]{1,0:T(8,128)(2,1)} async-done(((bf16[512,5120]{1,0:T(8,128)(2,1)}), bf16[16,5120]{1,0:T(8,128)(2,1)}) %reduce-scatter.8.cloned.1.call-update) | async-done | bytes 163856 | tf_op jit(solution)/shard_map/reduce_scatter | solution.py:100
  (45 shorter events, 0.3 us)
Async XLA Ops:
  7.2 7.6 %copy-start = (bf16[5120,128]{1,0:T(8,128)(2,1)S(1)}, bf16[5120,128]{1,0:T(8,128)(2,1)}, u32[]{:S(2)}) copy-start(bf16[5120,128]{1,0:T(8,128)(2,1)} %param.8) | copy-start | bytes 3932164
  7.2 5.1 %copy-start.7 = (bf16[5120,128]{1,0:T(8,128)(2,1)S(1)}, bf16[5120,128]{1,0:T(8,128)(2,1)}, u32[]{:S(2)}) copy-start(bf16[5120,128]{1,0:T(8,128)(2,1)} %param.9) | copy-start | bytes 3932164
  7.2 36.7 %all-gather.2.cloned.1.call-start = ((), (), s32[]{:S(2)}) async-start(), calls=%async_computation.3 | async-start | bytes 1179648 | tf_op jit(solution)/shard_map/all_gather | solution.py:57
  7.2 5.1 %copy-start.2 = (bf16[512,5120]{1,0:T(8,128)(2,1)S(1)}, bf16[512,5120]{1,0:T(8,128)(2,1)}, u32[]{:S(2)}) copy-start(bf16[512,5120]{1,0:T(8,128)(2,1)} %param.7) | copy-start | bytes 15728644
  11.8 7.0 %copy-start.11 = (bf16[512,128]{1,0:T(8,128)(2,1)}, bf16[512,128]{1,0:T(8,128)(2,1)S(1)}, u32[]{:S(2)}) copy-start(bf16[512,128]{1,0:T(8,128)(2,1)S(1)} %convolution_convert_fusion.7) | copy-start | bytes 393220
  11.8 14.6 %collective-permute-start.4 = (bf16[512,128]{1,0:T(8,128)(2,1)S(1)}, bf16[512,128]{1,0:T(8,128)(2,1)S(1)}, u32[]{:S(2)}, u32[]{:S(2)}) collective-permute-start(bf16[512,128]{1,0:T(8,128)(2,1)S(1)} %convolution_convert_fusion.7), channel_id=1, source_target_pairs={{32,0},{64,32},{96,64},{128,96},{160,128},{192,160},{224,192},{0,2... | collective-permute-start | bytes 393224 | tf_op jit(solution)/shard_map/ppermute | solution.py:47
  11.8 7.0 %collective-permute-start = (bf16[512,128]{1,0:T(8,128)(2,1)S(1)}, bf16[512,128]{1,0:T(8,128)(2,1)S(1)}, u32[]{:S(2)}, u32[]{:S(2)}) collective-permute-start(bf16[512,128]{1,0:T(8,128)(2,1)S(1)} %convolution_convert_fusion.7), channel_id=1, source_target_pairs={{0,32},{32,64},{64,96},{96,128},{128,160},{160,192},{192,224},{224... | collective-permute-start | bytes 393224 | tf_op jit(solution)/shard_map/ppermute | solution.py:44
  14.5 89.0 %reduce-scatter.6.cloned.1.call-start = ((), (), s32[]{:S(2)}) async-start(), calls=%async_computation.4 | async-start | bytes 2359296 | tf_op jit(solution)/shard_map/reduce_scatter | solution.py:77
  18.8 13.5 %copy-start.14 = (bf16[512,128]{1,0:T(8,128)(2,1)}, bf16[512,128]{1,0:T(8,128)(2,1)S(1)}, u32[]{:S(2)}) copy-start(bf16[512,128]{1,0:T(8,128)(2,1)S(1)} %collective-permute-done) | copy-start | bytes 393220
  18.8 17.7 %copy-start.12 = (bf16[512,128]{1,0:T(8,128)(2,1)S(1)}, bf16[512,128]{1,0:T(8,128)(2,1)}, u32[]{:S(2)}) copy-start(bf16[512,128]{1,0:T(8,128)(2,1)} %copy-done.11) | copy-start | bytes 393220
  18.8 7.0 %collective-permute-start.1 = (bf16[512,128]{1,0:T(8,128)(2,1)S(1)}, bf16[512,128]{1,0:T(8,128)(2,1)S(1)}, u32[]{:S(2)}, u32[]{:S(2)}) collective-permute-start(bf16[512,128]{1,0:T(8,128)(2,1)S(1)} %collective-permute-done), channel_id=1, source_target_pairs={{0,32},{32,64},{64,96},{96,128},{128,160},{160,192},{192,224},{224... | collective-permute-start | bytes 393224 | tf_op jit(solution)/shard_map/ppermute | solution.py:44
  25.8 4.4 %collective-permute-start.2 = (bf16[512,128]{1,0:T(8,128)(2,1)S(1)}, bf16[512,128]{1,0:T(8,128)(2,1)S(1)}, u32[]{:S(2)}, u32[]{:S(2)}) collective-permute-start(bf16[512,128]{1,0:T(8,128)(2,1)S(1)} %collective-permute-done.1), channel_id=1, source_target_pairs={{0,32},{32,64},{64,96},{96,128},{128,160},{160,192},{192,224},{224... | collective-permute-start | bytes 393224 | tf_op jit(solution)/shard_map/ppermute | solution.py:44
  26.4 6.0 %copy-start.13 = (bf16[512,128]{1,0:T(8,128)(2,1)}, bf16[512,128]{1,0:T(8,128)(2,1)S(1)}, u32[]{:S(2)}) copy-start(bf16[512,128]{1,0:T(8,128)(2,1)S(1)} %collective-permute-done.4) | copy-start | bytes 393220
  26.4 3.9 collective-permute-start.5
  30.2 5.3 %collective-permute-start.3 = (bf16[512,128]{1,0:T(8,128)(2,1)S(1)}, bf16[512,128]{1,0:T(8,128)(2,1)S(1)}, u32[]{:S(2)}, u32[]{:S(2)}) collective-permute-start(bf16[512,128]{1,0:T(8,128)(2,1)S(1)} %collective-permute-done.2), channel_id=1, source_target_pairs={{0,32},{32,64},{64,96},{96,128},{128,160},{160,192},{192,224},{224... | collective-permute-start | bytes 393224 | tf_op jit(solution)/shard_map/ppermute | solution.py:44
  30.3 7.3 %collective-permute-start.6 = (bf16[512,128]{1,0:T(8,128)(2,1)S(1)}, bf16[512,128]{1,0:T(8,128)(2,1)S(1)}, u32[]{:S(2)}, u32[]{:S(2)}) collective-permute-start(bf16[512,128]{1,0:T(8,128)(2,1)S(1)} %collective-permute-done.5), channel_id=1, source_target_pairs={{32,0},{64,32},{96,64},{128,96},{160,128},{192,160},{224,192},{0,2... | collective-permute-start | bytes 393224 | tf_op jit(solution)/shard_map/ppermute | solution.py:47
  38.3 10.5 %copy-start.5 = (bf16[8,512,128]{2,1,0:T(8,128)(2,1)}, bf16[8,512,128]{2,1,0:T(8,128)(2,1)S(1)}, u32[]{:S(2)}) copy-start(bf16[8,512,128]{2,1,0:T(8,128)(2,1)S(1)} %gather_fusion) | copy-start | bytes 3145732
  46.6 2.2 copy-start.10
  53.7 3.2 copy-start.1
  65.0 2.0 copy-start.3
  69.3 93.8 %reduce-scatter.10.cloned.1.call-start = ((), (), s32[]{:S(2)}) async-start(), calls=%async_computation.6 | async-start | bytes 5898240
  103.6 3.5 copy-start.6
  107.1 3.5 copy-start.4
  122.0 1.6 copy-start.8
  122.0 274.5 %reduce-scatter.8.cloned.1.call-start = ((), (), s32[]{:S(2)}) async-start(), calls=%async_computation.5 | async-start | bytes 5406720 | tf_op jit(solution)/shard_map/reduce_scatter | solution.py:100
  123.6 5.6 %copy-start.9 = (bf16[5120,128]{1,0:T(8,128)(2,1)S(1)}, bf16[5120,128]{1,0:T(8,128)(2,1)}, u32[]{:S(2)}) copy-start(bf16[5120,128]{1,0:T(8,128)(2,1)} %param.10) | copy-start | bytes 3932164
Sparse Core Ops, SparseCore 0:
  14.7 29.2 all-gather.1
  69.4 34.1 reduce-scatter.5
  122.1 40.9 reduce-scatter.9
  167.5 229.0 reduce-scatter.7
